TPU v7x, 128 devices: a whole 4x4x4 slice. The times are simulated.
128 devices in a mesh: dp: 8 (over x, y_hi), mp: 16 (over y_lo, z, core).
Axes of the slice: x: 4, y: 4 (y_hi: 2, y_lo: 2; y = y_hi * 2 + y_lo), z: 4, core: 2. Of those that a mesh axis runs over, the one named last changes fastest.
Arguments:
- tokens_in: bfloat16 [8192, 4096], P('dp', 'mp'), may hold values from -6 to 6
- grad_out: bfloat16 [8192, 14336], P('dp', 'mp'), may hold values from -6 to 6
- old_first: float32 [32, 128, 14336], P(None, ('dp', 'mp')), may hold values from -2 to 2
- old_second: float32 [32, 128, 14336], P(None, ('dp', 'mp')), may hold values from 0.01 to 1
- old_master: float32 [32, 128, 14336], P(None, ('dp', 'mp')), may hold values from -6 to 6
- step_count: int32 [1], replicated, may hold values from 1 to 31
Outputs:
- new_first: float32 [4096, 14336], P('dp', 'mp')
- new_second: float32 [4096, 14336], P('dp', 'mp')
- new_weights: float32 [4096, 14336], P(None, 'mp')
All inputs are finite; a program needn't handle non-finite values.
Results may differ from a plain program's by a relative error of at most 0.0003.
Values may be sent and summed in bfloat16 or wider, within the bound.
No kernel may reach another device: no remote copies, remote signals or barrier semaphores. Data moves between devices by JAX's collectives and lax.ppermute only.
A program may use at most 128 MiB of HBM per device.

v0:
```python
import math

import jax
import jax.numpy as jnp
from jax import lax
from jax.experimental import pallas as pl
from jax.experimental.pallas import tpu as pltpu
from jax.sharding import PartitionSpec as P


X = 4
HALF = 2
FIRST_UNIT = 2.0**14
SECOND_UNIT = 2.0**15
MASTER_UNIT = 2.0**13
REST_UNIT = 2.0**11
GRAD_UNIT = 2.0
WEIGHT_UNIT = 2.0**12


def dp_at(x, yh):
    return (x % X) * HALF + yh


EAST = [(dp_at(x, h), dp_at(x + 1, h)) for x in range(X) for h in range(HALF)]
WEST = [(dp_at(x, h), dp_at(x - 1, h)) for x in range(X) for h in range(HALF)]
ACROSS = [(dp_at(x, h), dp_at(x, 1 - h)) for x in range(X) for h in range(HALF)]


def token_moves():
    moves = []
    for src_x in range(X):
        for yh in range(HALF):
            for mp in range(16):
                yl, z, core = mp // 8, (mp // 2) % 4, mp % 2
                dst_x = 2 * yl + z // 2
                step = (src_x - dst_x) % X
                slot = step * 4 + ((z % 2) ^ yh) * 2 + core
                moves.append((dp_at(src_x, yh) * 16 + mp, dp_at(dst_x, yh) * 16 + slot))
    return moves


def east(value):
    return lax.ppermute(value, "dp", EAST)


def west(value):
    return lax.ppermute(value, "dp", WEST)


def across(value):
    return lax.ppermute(value, "dp", ACROSS)


def place(rows, pieces, out, shape):
    count = len(pieces)

    def body(row_ref, *refs):
        copies = []
        for n in range(count):
            size = pieces[n].shape[0]
            row = pl.multiple_of(row_ref[n], size)
            copies.append(pltpu.make_async_copy(refs[n], refs[-2].at[pl.ds(row, size)], refs[-1].at[n]))
        for copy in copies:
            copy.start()
        for copy in copies:
            copy.wait()

    anywhere = pl.BlockSpec(memory_space=pl.ANY)
    held = [] if out is None else [out]
    return pl.pallas_call(
        body,
        out_shape=jax.ShapeDtypeStruct(shape, jnp.float32),
        in_specs=[
            pl.BlockSpec(memory_space=pltpu.SMEM),
            *[pl.BlockSpec(memory_space=pltpu.VMEM)] * count,
            *[anywhere] * len(held),
        ],
        out_specs=pl.BlockSpec(memory_space=pltpu.HBM),
        scratch_shapes=[pltpu.SemaphoreType.DMA((count,))],
        input_output_aliases={count + 1: 0} if held else {},
    )(rows, *pieces, *held)


def settle(out):
    return pl.pallas_call(
        lambda out_ref, same_ref: None,
        out_shape=jax.ShapeDtypeStruct(out.shape, out.dtype),
        in_specs=[pl.BlockSpec(memory_space=pltpu.HBM)],
        out_specs=pl.BlockSpec(memory_space=pltpu.HBM),
        input_output_aliases={0: 0},
    )(out)


def local(tokens_in, grad_out, old_first, old_second, old_master, step_count):
    dp_count = lax.axis_size("dp")
    mp_count = lax.axis_size("mp")
    device_total = dp_count * mp_count
    tok_rows = tokens_in.shape[0]
    col_width = grad_out.shape[1]
    grad_scale = 1.0 / math.sqrt(tok_rows * dp_count)
    run_rows = old_first.shape[0] // dp_count
    half = tok_rows // 2
    block = run_rows * device_total

    tokens = lax.ppermute(tokens_in, ("dp", "mp"), token_moves())
    west_top = east(grad_out[:half])
    east_bottom = west(grad_out[half:])
    west_bottom = east(grad_out[half:])
    east_top = west(grad_out[:half])
    tokens = lax.all_gather(tokens, "mp", axis=1, tiled=True)
    far_top = east(west_top)
    far_bottom = west(east_bottom)
    far_group = lax.optimization_barrier(jnp.concatenate([far_top, far_bottom]))
    from_west = lax.optimization_barrier(jnp.concatenate([west_top, west_bottom]))
    from_east = lax.optimization_barrier(jnp.concatenate([east_top, east_bottom]))

    flat = [
        lax.optimization_barrier(state.reshape(dp_count * run_rows, -1))
        for state in (old_first, old_second, old_master)
    ]
    lead = (flat[0] * FIRST_UNIT).astype(jnp.float16)
    scaled = flat[2] * MASTER_UNIT
    high = lax.reduce_precision(scaled, 5, 10)
    units = [
        lead,
        (flat[1] * SECOND_UNIT).astype(jnp.float16),
        high.astype(jnp.float16),
        ((scaled - high) * REST_UNIT).astype(jnp.float16),
    ]
    parts = [unit.reshape(dp_count, run_rows, mp_count, col_width) for unit in units]
    packed = jnp.concatenate(parts, axis=3).transpose(1, 0, 2, 3)
    packed = packed.reshape(run_rows, device_total, len(units) * col_width)
    moved = lax.all_to_all(packed, ("dp", "mp"), split_axis=1, concat_axis=1, tiled=True)
    moved = [
        moved[:, :, n * col_width : (n + 1) * col_width].astype(jnp.float32).reshape(block, col_width)
        for n in range(len(units))
    ]

    def product(own):
        total = None
        for step, rows, values in (
            (0, slice(None), grad_out),
            (1, slice(None), from_east),
            (3, slice(None), from_west),
            (2, slice(None), far_group),
        ):
            start = (step * 4 + own * 2) * 256
            left = tokens[rows, start : start + block]
            dot = lax.dot_general(left, values, (((0,), (0,)), ((), ())), preferred_element_type=jnp.float32)
            total = dot if total is None else total + dot
        return total * grad_scale

    other = (product(1) * GRAD_UNIT).astype(jnp.float16)
    other = across(other)
    mine = lax.optimization_barrier(product(0))
    grad = mine + other.astype(jnp.float32) * (1.0 / GRAD_UNIT)
    first = moved[0] * (1.0 / FIRST_UNIT)
    second = moved[1] * (1.0 / SECOND_UNIT)
    master = (moved[2] + moved[3] * (1.0 / REST_UNIT)) * (1.0 / MASTER_UNIT)
    step_float = step_count[0].astype(jnp.float32)
    correct_one = 1.0 - jnp.power(jnp.float32(0.9), step_float)
    correct_two = 1.0 - jnp.power(jnp.float32(0.95), step_float)
    new_first = 0.9 * first + 0.1 * grad
    new_second = 0.95 * second + 0.05 * grad * grad
    update = new_first / correct_one / (jnp.sqrt(new_second / correct_two) + 1e-08)
    new_master = master - 0.02 * (update + 0.1 * master)
    own = lax.optimization_barrier((new_master * WEIGHT_UNIT).astype(jnp.float16))
    mid = block // 2
    west_row = east(own)
    east_row = west(own)
    pair = across(own)
    far_one = east(west_row[:mid])
    far_two = west(east_row[mid:])
    west_pair = east(pair)
    east_pair = west(pair)
    far_pair_one = across(far_one)
    far_pair_two = across(far_two)
    here = lax.axis_index("dp")

    def spot(dx, flip):
        return (((here + dx * HALF) & (dp_count - 1)) ^ flip) * block

    def wide(values):
        return values.astype(jnp.float32) * (1.0 / WEIGHT_UNIT)

    out = place(spot(0, 0)[None], [wide(own)], None, (dp_count * block, col_width))
    for wave in (
        ((west_row, 3, 0, 0), (east_row, 1, 0, 0)),
        ((pair, 0, 1, 0), (far_one, 2, 0, 0), (far_two, 2, 0, mid)),
        ((west_pair, 3, 1, 0), (east_pair, 1, 1, 0)),
        ((far_pair_one, 2, 1, 0), (far_pair_two, 2, 1, mid)),
    ):
        for values, dx, flip, at in wave:
            out = lax.dynamic_update_slice(out, wide(values), (spot(dx, flip) + at, 0))
    out = settle(out)
    return (new_first, new_second, out)


def solution(mesh):
    placed = (
        P("dp", "mp"),
        P("dp", "mp"),
        P(None, ("dp", "mp"), None),
        P(None, ("dp", "mp"), None),
        P(None, ("dp", "mp"), None),
        P(),
    )
    return jax.shard_map(
        local,
        mesh=mesh,
        in_specs=placed,
        out_specs=(P("dp", "mp"), P("dp", "mp"), P(None, "mp")),
        check_vma=False,
    )
```

profile of v0, /device:TPU:0, one launch (start us, length us, event | category | flops | bytes accessed | tf_op | source)
XLA Modules:
  0.0 272.1 jit_solution(10082662838195292131)
XLA Ops:
  7.2 1.7 collective-permute-start
  9.7 2.1 copy.71
  19.1 4.1 %pad_maximum_fusion = f16[8,4,16,3584]{3,1,2,0:T(4,128)(2,1)} fusion(f16[8,4,16,896]{3,1,2,0:T(4,128)(2,1)S(1)} %copy.34, f16[8,4,16,896]{3,1,2,0:T(4,128)(2,1)S(1)} %copy.33, f16[8,4,16,896]{3,1,2,0:T(4,128)(2,1)S(1)} %copy.32, f16[8,4,16,896]{3,1,2,0:T(4,128)(2,1)S(1)} %copy.31), kind=kLoop, calls=%fused_computation | loop fusion | flops 5505024 | bytes 7340032 | tf_op jit(solution)/shard_map/concatenate | solution.py:132
  23.2 38.4 %all-to-all-start = ((f16[4,128,3584]{2,0,1:T(4,128)(2,1)}), f16[4,128,3584]{2,0,1:T(4,128)(2,1)}, u32[]{:S(2)}, u32[]{:S(2)}) async-start(f16[4,128,3584]{2,0,1:T(4,128)(2,1)} %bitcast.79), calls=%async_computation | async-start | bytes 7340032 | tf_op jit(solution)/shard_map/all_to_all | solution.py:134
  61.8 2.2 collective-permute-start.2
  64.8 2.4 collective-permute-start.1
  67.2 54.7 %collective-permute-done.2 = bf16[512,896]{1,0:T(8,128)(2,1)S(1)} collective-permute-done((bf16[512,896]{1,0:T(8,128)(2,1)S(1)}, bf16[512,896]{1,0:T(8,128)(2,1)S(1)}, u32[]{:S(2)}, u32[]{:S(2)}) %collective-permute-start.2) | collective-permute-done | bytes 917536 | tf_op jit(solution)/shard_map/ppermute | solution.py:48
  122.0 2.2 collective-permute-start.6
  124.9 17.8 %collective-permute-done.4 = bf16[512,896]{1,0:T(8,128)(2,1)S(1)} collective-permute-done((bf16[512,896]{1,0:T(8,128)(2,1)S(1)}, bf16[512,896]{1,0:T(8,128)(2,1)S(1)}, u32[]{:S(2)}, u32[]{:S(2)}) %collective-permute-start.4) | collective-permute-done | bytes 917536 | tf_op jit(solution)/shard_map/ppermute | solution.py:44
  142.6 1.4 pad_maximum_fusion.2
  145.5 15.3 %collective-permute-done.6 = bf16[512,896]{1,0:T(8,128)(2,1)S(1)} collective-permute-done((bf16[512,896]{1,0:T(8,128)(2,1)S(1)}, bf16[512,896]{1,0:T(8,128)(2,1)S(1)}, u32[]{:S(2)}, u32[]{:S(2)}) %collective-permute-start.6) | collective-permute-done | bytes 917536 | tf_op jit(solution)/shard_map/ppermute | solution.py:48
  162.1 3.5 %fusion.27 = (f16[4,128,896]{2,0,1:T(4,128)(2,1)S(1)}, f16[4,128,896]{2,0,1:T(4,128)(2,1)S(1)}, f16[4,128,896]{2,0,1:T(4,128)(2,1)S(1)}, f16[4,128,896]{2,0,1:T(4,128)(2,1)S(1)}) fusion(f16[4,128,3584]{2,0,1:T(4,128)(2,1)} %all-to-all-done), kind=kLoop, calls=%fused_computation.60 | loop fusion | bytes 7340032 | tf_op jit(solution)/shard_map/slice | solution.py:136
  165.5 2.4 fusion.11
  167.9 2.3 convert_multiply_fusion.1
  170.2 3.2 %fusion.17 = f32[512,896]{1,0:T(8,128)S(1)} fusion(bf16[1024,896]{1,0:T(8,128)(2,1)} %param.7, bf16[1024,4096]{1,0:T(8,128)(2,1)} %all-gather.2.cloned.1.call-done), kind=kOutput, calls=%fused_computation.47 | convolution fusion | flops 939524096 | bytes 4718592 | tf_op jit(solution)/shard_map/dot_general | solution.py:150
  173.5 3.2 %fusion.13 = f32[896,512]{0,1:T(8,128)S(1)} fusion(bf16[1024,896]{1,0:T(8,128)(2,1)} %pad_maximum_fusion.2, bf16[1024,4096]{1,0:T(8,128)(2,1)} %all-gather.2.cloned.1.call-done), kind=kOutput, calls=%fused_computation.43 | convolution fusion | flops 939524096 | bytes 4718592 | tf_op jit(solution)/shard_map/dot_general | solution.py:150
  178.0 1.4 fusion.8
  179.5 3.3 %collective-permute-start.7 = (f16[512,896]{1,0:T(8,128)(2,1)S(1)}, f16[512,896]{1,0:T(8,128)(2,1)S(1)}, u32[]{:S(2)}, u32[]{:S(2)}) collective-permute-start(f16[512,896]{1,0:T(8,128)(2,1)S(1)} %fusion.8), channel_id=1, source_target_pairs={{0,16},{16,0},{32,48},{48,32},{64,80},{80,64},{96,112},{112,96},{1... | collective-permute-start | bytes 2752520 | tf_op jit(solution)/shard_map/ppermute | solution.py:52
  188.1 15.1 %collective-permute-done.7 = f16[512,896]{1,0:T(8,128)(2,1)S(1)} collective-permute-done((f16[512,896]{1,0:T(8,128)(2,1)S(1)}, f16[512,896]{1,0:T(8,128)(2,1)S(1)}, u32[]{:S(2)}, u32[]{:S(2)}) %collective-permute-start.7) | collective-permute-done | bytes 917536 | tf_op jit(solution)/shard_map/ppermute | solution.py:52
  203.3 3.3 %fusion.6 = (f16[512,896]{1,0:T(8,128)(2,1)S(1)}, f32[512,896]{1,0:T(8,128)}, f32[512,896]{1,0:T(8,128)}) fusion(f32[4,128,896]{2,1,0:T(8,128)S(1)} %copy-done.3, f32[4,128,896]{2,1,0:T(8,128)S(1)} %copy-done.2, f32[]{:T(128)} %bitcast.13, f32[]{:T(128)} %bitcast.12, f32[512,896]{1,0:T(8,128)S(1)} %fusion.9, f16[512,896]{1,0:T(8,128)(2,1)S(1)} %collective-permute-done.7, ...), kind=kLoop, calls=%fused_computation.17 | loop fusion | flops 7798784 | bytes 14680072 | tf_op jit(solution)/shard_map/convert_element_type | solution.py:168
  206.7 3.2 %collective-permute-start.9 = (f16[512,896]{1,0:T(8,128)(2,1)S(1)}, f16[512,896]{1,0:T(8,128)(2,1)S(1)}, u32[]{:S(2)}, u32[]{:S(2)}) collective-permute-start(f16[512,896]{1,0:T(8,128)(2,1)S(1)} %get-tuple-element.3), channel_id=1, source_target_pairs={{0,96},{16,112},{32,0},{48,16},{64,32},{80,48},{96,64},{112,80},{1... | collective-permute-start | bytes 2752520 | tf_op jit(solution)/shard_map/ppermute | solution.py:48
  209.8 3.0 %collective-permute-start.10 = (f16[512,896]{1,0:T(8,128)(2,1)S(1)}, f16[512,896]{1,0:T(8,128)(2,1)}, u32[]{:S(2)}, u32[]{:S(2)}) collective-permute-start(f16[512,896]{1,0:T(8,128)(2,1)S(1)} %get-tuple-element.3), channel_id=1, source_target_pairs={{0,16},{16,0},{32,48},{48,32},{64,80},{80,64},{96,112},{112,96},{1... | collective-permute-start | bytes 2752520 | tf_op jit(solution)/shard_map/ppermute | solution.py:52
  212.9 1.4 convert_multiply_fusion.refs_0_
  214.3 2.7 %shard_map.85 = f32[4096,896]{1,0:T(8,128)} custom-call(s32[1]{0:T(128)} %bitcast.10.row_ref, f32[512,896]{1,0:T(8,128)} %convert_multiply_fusion.refs_0_), custom_call_target="tpu_custom_call" | custom-call | tf_op jit(solution)/shard_map/pallas_call | solution.py:71
  217.0 11.9 %collective-permute-done.8 = f16[512,896]{1,0:T(8,128)(2,1)S(1)} collective-permute-done((f16[512,896]{1,0:T(8,128)(2,1)S(1)}, f16[512,896]{1,0:T(8,128)(2,1)S(1)}, u32[]{:S(2)}, u32[]{:S(2)}) %collective-permute-start.8) | collective-permute-done | bytes 917536 | tf_op jit(solution)/shard_map/ppermute | solution.py:44
  229.2 3.3 %collective-permute-start.12 = (f16[256,896]{1,0:T(8,128)(2,1)S(1)}, f16[256,896]{1,0:T(8,128)(2,1)S(1)}, u32[]{:S(2)}, u32[]{:S(2)}) collective-permute-start(f16[256,896]{1,0:T(8,128)(2,1)S(1)} %slice.79), channel_id=1, source_target_pairs={{0,96},{16,112},{32,0},{48,16},{64,32},{80,48},{96,64},{112,80},{1... | collective-permute-start | bytes 1376264 | tf_op jit(solution)/shard_map/ppermute | solution.py:48
  232.5 3.2 %collective-permute-start.14 = (f16[512,896]{1,0:T(8,128)(2,1)}, f16[512,896]{1,0:T(8,128)(2,1)S(1)}, u32[]{:S(2)}, u32[]{:S(2)}) collective-permute-start(f16[512,896]{1,0:T(8,128)(2,1)} %collective-permute-done.10), channel_id=1, source_target_pairs={{0,96},{16,112},{32,0},{48,16},{64,32},{80,48},{96,64},{112,80},{1... | collective-permute-start | bytes 2752520 | tf_op jit(solution)/shard_map/ppermute | solution.py:48
  238.5 2.6 multiply_dynamic-update-slice_fusion.2
  241.1 2.6 collective-permute-done.11
  243.7 3.0 %collective-permute-start.15 = (f16[256,896]{1,0:T(8,128)(2,1)S(1)}, f16[256,896]{1,0:T(8,128)(2,1)S(1)}, u32[]{:S(2)}, u32[]{:S(2)}) collective-permute-start(f16[256,896]{1,0:T(8,128)(2,1)S(1)} %collective-permute-done.11), channel_id=1, source_target_pairs={{0,16},{16,0},{32,48},{48,32},{64,80},{80,64},{96,112},{112,96},{1... | collective-permute-start | bytes 1376264 | tf_op jit(solution)/shard_map/ppermute | solution.py:52
  249.2 11.3 %collective-permute-done.13 = f16[512,896]{1,0:T(8,128)(2,1)S(1)} collective-permute-done((f16[512,896]{1,0:T(8,128)(2,1)}, f16[512,896]{1,0:T(8,128)(2,1)S(1)}, u32[]{:S(2)}, u32[]{:S(2)}) %collective-permute-start.13) | collective-permute-done | bytes 917536 | tf_op jit(solution)/shard_map/ppermute | solution.py:44
  261.9 1.4 multiply_dynamic-update-slice_fusion
  (76 shorter events, 27.3 us)
Async XLA Ops:
  7.2 163.1 %all-gather.2.cloned.1.call-start = ((), (), s32[]{:S(2)}) async-start(), calls=%async_computation.1 | async-start | bytes 8912896 | tf_op jit(solution)/shard_map/all_gather | solution.py:111
  7.2 1.7 collective-permute-start
  8.9 0.8 copy-start.11
  13.8 1.5 copy-start.7
  16.0 1.5 copy-start.8
  23.2 38.4 %copy-start = (bf16[1024,896]{1,0:T(8,128)(2,1)S(1)}, bf16[1024,896]{1,0:T(8,128)(2,1)}, u32[]{:S(2)}) copy-start(bf16[1024,896]{1,0:T(8,128)(2,1)} %param.7) | copy-start | bytes 5505028
  23.2 138.9 %all-to-all-start = ((f16[4,128,3584]{2,0,1:T(4,128)(2,1)}), f16[4,128,3584]{2,0,1:T(4,128)(2,1)}, u32[]{:S(2)}, u32[]{:S(2)}) async-start(f16[4,128,3584]{2,0,1:T(4,128)(2,1)} %bitcast.79), calls=%async_computation | async-start | bytes 7340032 | tf_op jit(solution)/shard_map/all_to_all | solution.py:134
  61.8 60.2 %collective-permute-start.2 = (bf16[512,896]{1,0:T(8,128)(2,1)S(1)}, bf16[512,896]{1,0:T(8,128)(2,1)S(1)}, u32[]{:S(2)}, u32[]{:S(2)}) collective-permute-start(bf16[512,896]{1,0:T(8,128)(2,1)S(1)} %get-tuple-element.11), channel_id=1, source_target_pairs={{0,96},{16,112},{32,0},{48,16},{64,32},{80,48},{96,64},{112,80},{1... | collective-permute-start | bytes 2752520 | tf_op jit(solution)/shard_map/ppermute | solution.py:48
  63.9 60.2 %collective-permute-start.3 = (bf16[512,896]{1,0:T(8,128)(2,1)S(1)}, bf16[512,896]{1,0:T(8,128)(2,1)S(1)}, u32[]{:S(2)}, u32[]{:S(2)}) collective-permute-start(bf16[512,896]{1,0:T(8,128)(2,1)S(1)} %get-tuple-element.10), channel_id=1, source_target_pairs={{0,32},{16,48},{32,64},{48,80},{64,96},{80,112},{96,0},{112,16},{1... | collective-permute-start | bytes 2752520 | tf_op jit(solution)/shard_map/ppermute | solution.py:44
  64.0 78.7 %collective-permute-start.4 = (bf16[512,896]{1,0:T(8,128)(2,1)S(1)}, bf16[512,896]{1,0:T(8,128)(2,1)S(1)}, u32[]{:S(2)}, u32[]{:S(2)}) collective-permute-start(bf16[512,896]{1,0:T(8,128)(2,1)S(1)} %get-tuple-element.11), channel_id=1, source_target_pairs={{0,32},{16,48},{32,64},{48,80},{64,96},{80,112},{96,0},{112,16},{1... | collective-permute-start | bytes 2752520 | tf_op jit(solution)/shard_map/ppermute | solution.py:44
  64.8 79.3 %collective-permute-start.1 = (bf16[512,896]{1,0:T(8,128)(2,1)S(1)}, bf16[512,896]{1,0:T(8,128)(2,1)S(1)}, u32[]{:S(2)}, u32[]{:S(2)}) collective-permute-start(bf16[512,896]{1,0:T(8,128)(2,1)S(1)} %get-tuple-element.10), channel_id=1, source_target_pairs={{0,96},{16,112},{32,0},{48,16},{64,32},{80,48},{96,64},{112,80},{1... | collective-permute-start | bytes 2752520 | tf_op jit(solution)/shard_map/ppermute | solution.py:48
  122.0 38.8 %collective-permute-start.6 = (bf16[512,896]{1,0:T(8,128)(2,1)S(1)}, bf16[512,896]{1,0:T(8,128)(2,1)S(1)}, u32[]{:S(2)}, u32[]{:S(2)}) collective-permute-start(bf16[512,896]{1,0:T(8,128)(2,1)S(1)} %collective-permute-done.2), channel_id=1, source_target_pairs={{0,96},{16,112},{32,0},{48,16},{64,32},{80,48},{96,64},{112,80},{1... | collective-permute-start | bytes 2752520 | tf_op jit(solution)/shard_map/ppermute | solution.py:48
  124.1 37.8 %collective-permute-start.5 = (bf16[512,896]{1,0:T(8,128)(2,1)S(1)}, bf16[512,896]{1,0:T(8,128)(2,1)S(1)}, u32[]{:S(2)}, u32[]{:S(2)}) collective-permute-start(bf16[512,896]{1,0:T(8,128)(2,1)S(1)} %collective-permute-done.3), channel_id=1, source_target_pairs={{0,32},{16,48},{32,64},{48,80},{64,96},{80,112},{96,0},{112,16},{1... | collective-permute-start | bytes 2752520 | tf_op jit(solution)/shard_map/ppermute | solution.py:44
  170.2 6.5 %copy-start.6 = (bf16[1024,4096]{1,0:T(8,128)(2,1)S(1)}, bf16[1024,4096]{1,0:T(8,128)(2,1)}, u32[]{:S(2)}) copy-start(bf16[1024,4096]{1,0:T(8,128)(2,1)} %all-gather.2.cloned.1.call-done) | copy-start | bytes 25165828
  173.5 3.2 %copy-start.10 = (bf16[1024,896]{1,0:T(8,128)(2,1)S(1)}, bf16[1024,896]{1,0:T(8,128)(2,1)}, u32[]{:S(2)}) copy-start(bf16[1024,896]{1,0:T(8,128)(2,1)} %pad_maximum_fusion.1) | copy-start | bytes 5505028
  178.0 4.8 %copy-start.9 = (bf16[1024,896]{1,0:T(8,128)(2,1)S(1)}, bf16[1024,896]{1,0:T(8,128)(2,1)}, u32[]{:S(2)}) copy-start(bf16[1024,896]{1,0:T(8,128)(2,1)} %pad_maximum_fusion.2) | copy-start | bytes 5505028
  179.5 4.6 %copy-start.1 = (bf16[1024,896]{1,0:T(8,128)(2,1)S(1)}, bf16[1024,896]{1,0:T(8,128)(2,1)}, u32[]{:S(2)}) copy-start(bf16[1024,896]{1,0:T(8,128)(2,1)} %param.7) | copy-start | bytes 5505028
  179.5 23.8 %collective-permute-start.7 = (f16[512,896]{1,0:T(8,128)(2,1)S(1)}, f16[512,896]{1,0:T(8,128)(2,1)S(1)}, u32[]{:S(2)}, u32[]{:S(2)}) collective-permute-start(f16[512,896]{1,0:T(8,128)(2,1)S(1)} %fusion.8), channel_id=1, source_target_pairs={{0,16},{16,0},{32,48},{48,32},{64,80},{80,64},{96,112},{112,96},{1... | collective-permute-start | bytes 2752520 | tf_op jit(solution)/shard_map/ppermute | solution.py:52
  186.7 16.5 %copy-start.2 = (f32[4,128,896]{2,1,0:T(8,128)S(1)}, f32[4,128,896]{2,1,0:T(8,128)}, u32[]{:S(2)}) copy-start(f32[4,128,896]{2,1,0:T(8,128)} %get-tuple-element.12) | copy-start | bytes 5505028
  186.7 16.5 %copy-start.3 = (f32[4,128,896]{2,1,0:T(8,128)S(1)}, f32[4,128,896]{2,1,0:T(8,128)}, u32[]{:S(2)}) copy-start(f32[4,128,896]{2,1,0:T(8,128)} %get-tuple-element.13) | copy-start | bytes 5505028
  186.7 16.5 %copy-start.4 = (f32[4,128,896]{2,1,0:T(8,128)S(1)}, f32[4,128,896]{2,1,0:T(8,128)}, u32[]{:S(2)}) copy-start(f32[4,128,896]{2,1,0:T(8,128)} %get-tuple-element.16) | copy-start | bytes 5505028
  186.8 16.5 %copy-start.5 = (f32[4,128,896]{2,1,0:T(8,128)S(1)}, f32[4,128,896]{2,1,0:T(8,128)}, u32[]{:S(2)}) copy-start(f32[4,128,896]{2,1,0:T(8,128)} %get-tuple-element.17) | copy-start | bytes 5505028
  206.6 22.3 %collective-permute-start.8 = (f16[512,896]{1,0:T(8,128)(2,1)S(1)}, f16[512,896]{1,0:T(8,128)(2,1)S(1)}, u32[]{:S(2)}, u32[]{:S(2)}) collective-permute-start(f16[512,896]{1,0:T(8,128)(2,1)S(1)} %get-tuple-element.3), channel_id=1, source_target_pairs={{0,32},{16,48},{32,64},{48,80},{64,96},{80,112},{96,0},{112,16},{1... | collective-permute-start | bytes 2752520 | tf_op jit(solution)/shard_map/ppermute | solution.py:44
  206.7 22.4 %collective-permute-start.9 = (f16[512,896]{1,0:T(8,128)(2,1)S(1)}, f16[512,896]{1,0:T(8,128)(2,1)S(1)}, u32[]{:S(2)}, u32[]{:S(2)}) collective-permute-start(f16[512,896]{1,0:T(8,128)(2,1)S(1)} %get-tuple-element.3), channel_id=1, source_target_pairs={{0,96},{16,112},{32,0},{48,16},{64,32},{80,48},{96,64},{112,80},{1... | collective-permute-start | bytes 2752520 | tf_op jit(solution)/shard_map/ppermute | solution.py:48
  209.8 22.6 %collective-permute-start.10 = (f16[512,896]{1,0:T(8,128)(2,1)S(1)}, f16[512,896]{1,0:T(8,128)(2,1)}, u32[]{:S(2)}, u32[]{:S(2)}) collective-permute-start(f16[512,896]{1,0:T(8,128)(2,1)S(1)} %get-tuple-element.3), channel_id=1, source_target_pairs={{0,16},{16,0},{32,48},{48,32},{64,80},{80,64},{96,112},{112,96},{1... | collective-permute-start | bytes 2752520 | tf_op jit(solution)/shard_map/ppermute | solution.py:52
  229.0 14.7 %collective-permute-start.11 = (f16[256,896]{1,0:T(8,128)(2,1)S(1)}, f16[256,896]{1,0:T(8,128)(2,1)S(1)}, u32[]{:S(2)}, u32[]{:S(2)}) collective-permute-start(f16[256,896]{1,0:T(8,128)(2,1)S(1)} %slice.78), channel_id=1, source_target_pairs={{0,32},{16,48},{32,64},{48,80},{64,96},{80,112},{96,0},{112,16},{1... | collective-permute-start | bytes 1376264 | tf_op jit(solution)/shard_map/ppermute | solution.py:44
  229.2 17.5 %collective-permute-start.12 = (f16[256,896]{1,0:T(8,128)(2,1)S(1)}, f16[256,896]{1,0:T(8,128)(2,1)S(1)}, u32[]{:S(2)}, u32[]{:S(2)}) collective-permute-start(f16[256,896]{1,0:T(8,128)(2,1)S(1)} %slice.79), channel_id=1, source_target_pairs={{0,96},{16,112},{32,0},{48,16},{64,32},{80,48},{96,64},{112,80},{1... | collective-permute-start | bytes 1376264 | tf_op jit(solution)/shard_map/ppermute | solution.py:48
  232.5 28.0 %collective-permute-start.13 = (f16[512,896]{1,0:T(8,128)(2,1)}, f16[512,896]{1,0:T(8,128)(2,1)S(1)}, u32[]{:S(2)}, u32[]{:S(2)}) collective-permute-start(f16[512,896]{1,0:T(8,128)(2,1)} %collective-permute-done.10), channel_id=1, source_target_pairs={{0,32},{16,48},{32,64},{48,80},{64,96},{80,112},{96,0},{112,16},{1... | collective-permute-start | bytes 2752520 | tf_op jit(solution)/shard_map/ppermute | solution.py:44
  232.5 29.4 %collective-permute-start.14 = (f16[512,896]{1,0:T(8,128)(2,1)}, f16[512,896]{1,0:T(8,128)(2,1)S(1)}, u32[]{:S(2)}, u32[]{:S(2)}) collective-permute-start(f16[512,896]{1,0:T(8,128)(2,1)} %collective-permute-done.10), channel_id=1, source_target_pairs={{0,96},{16,112},{32,0},{48,16},{64,32},{80,48},{96,64},{112,80},{1... | collective-permute-start | bytes 2752520 | tf_op jit(solution)/shard_map/ppermute | solution.py:48
  243.7 19.6 %collective-permute-start.15 = (f16[256,896]{1,0:T(8,128)(2,1)S(1)}, f16[256,896]{1,0:T(8,128)(2,1)S(1)}, u32[]{:S(2)}, u32[]{:S(2)}) collective-permute-start(f16[256,896]{1,0:T(8,128)(2,1)S(1)} %collective-permute-done.11), channel_id=1, source_target_pairs={{0,16},{16,0},{32,48},{48,32},{64,80},{80,64},{96,112},{112,96},{1... | collective-permute-start | bytes 1376264 | tf_op jit(solution)/shard_map/ppermute | solution.py:52
  246.7 17.6 %collective-permute-start.16 = (f16[256,896]{1,0:T(8,128)(2,1)S(1)}, f16[256,896]{1,0:T(8,128)(2,1)S(1)}, u32[]{:S(2)}, u32[]{:S(2)}) collective-permute-start(f16[256,896]{1,0:T(8,128)(2,1)S(1)} %collective-permute-done.12), channel_id=1, source_target_pairs={{0,16},{16,0},{32,48},{48,32},{64,80},{80,64},{96,112},{112,96},{1... | collective-permute-start | bytes 1376264 | tf_op jit(solution)/shard_map/ppermute | solution.py:52
Sparse Core Ops, SparseCore 0:
  9.9 129.5 all-gather.1
where the time goes:
time: 273 us; the launch traced here: 272 us
  waiting for transfers between devices  130 us (48%)
  starting transfers between devices  67.5 us (25%)
  other arithmetic  30.1 us (11%)
  between operations  15.1 us (6%)
  matrix products  14.4 us (5%)
  local copies, waits for them, and re-layouts  12.3 us (5%)
  Pallas kernels  2.73 us (1%)
    ppermute x6, waiting for transfers between devices, west(): return lax.ppermute(value, 'dp', WEST)  70 us
    ppermute x6, waiting for transfers between devices, east(): return lax.ppermute(value, 'dp', EAST)  44.8 us
    all_to_all x1, starting transfers between devices, local(): lax.all_to_all(packed, ('dp', 'mp'), split_axis=1, concat_axis=1, tiled=T...  38.4 us
    ppermute x6, starting transfers between devices, west(): return lax.ppermute(value, 'dp', WEST)  16.5 us
    ppermute x4, waiting for transfers between devices, across(): return lax.ppermute(value, 'dp', ACROSS)  15.1 us
    dot_general x8, matrix products, product(): lax.dot_general(left, values, (((0,), (0,)), ((), ())), preferred_element...  14.4 us
    dynamic_update_slice x9, other arithmetic, local(): out = lax.dynamic_update_slice(out, wide(values), (spot(dx, flip) + at, 0))  12.1 us
    ppermute x4, starting transfers between devices, across(): return lax.ppermute(value, 'dp', ACROSS)  9.86 us
  transfers between devices with their start and end apart: 19, of which 8 were waited for; matrix products, arithmetic and copies ran while one was open for 15% of the time, Pallas kernels for 1%

commit v1 on v0

--- a/solution.py
+++ b/solution.py
@@ -108,7 +108,8 @@
     east_bottom = west(grad_out[half:])
     west_bottom = east(grad_out[half:])
     east_top = west(grad_out[:half])
-    tokens = lax.all_gather(tokens, "mp", axis=1, tiled=True)
+    tokens = lax.all_gather(tokens, "mp", axis=0, tiled=True)
+    tokens = tokens.reshape(X, 4, tok_rows, -1)
     far_top = east(west_top)
     far_bottom = west(east_bottom)
     far_group = lax.optimization_barrier(jnp.concatenate([far_top, far_bottom]))
@@ -139,17 +140,11 @@
 
     def product(own):
         total = None
-        for step, rows, values in (
-            (0, slice(None), grad_out),
-            (1, slice(None), from_east),
-            (3, slice(None), from_west),
-            (2, slice(None), far_group),
-        ):
-            start = (step * 4 + own * 2) * 256
-            left = tokens[rows, start : start + block]
-            dot = lax.dot_general(left, values, (((0,), (0,)), ((), ())), preferred_element_type=jnp.float32)
+        for step, values in ((0, grad_out), (1, from_east), (3, from_west), (2, far_group)):
+            left = tokens[step, 2 * own : 2 * own + 2]
+            dot = lax.dot_general(left, values, (((1,), (0,)), ((), ())), preferred_element_type=jnp.float32)
             total = dot if total is None else total + dot
-        return total * grad_scale
+        return total.reshape(block, col_width) * grad_scale
 
     other = (product(1) * GRAD_UNIT).astype(jnp.float16)
     other = across(other)
@@ -166,6 +161,10 @@
     update = new_first / correct_one / (jnp.sqrt(new_second / correct_two) + 1e-08)
     new_master = master - 0.02 * (update + 0.1 * master)
     own = lax.optimization_barrier((new_master * WEIGHT_UNIT).astype(jnp.float16))
+    mine, other, first, second, _ = lax.optimization_barrier((mine, other, moved[0], moved[1], own))
+    grad = mine + other.astype(jnp.float32) * (1.0 / GRAD_UNIT)
+    new_first = 0.9 * (first * (1.0 / FIRST_UNIT)) + 0.1 * grad
+    new_second = 0.95 * (second * (1.0 / SECOND_UNIT)) + 0.05 * grad * grad
     mid = block // 2
     west_row = east(own)
     east_row = west(own)

time: 273 us -> 278 us (1.018)
  waiting for transfers between devices: 130 us -> 117 us
  other arithmetic: 30.1 us -> 43 us
  local copies, waits for them, and re-layouts: 12.3 us -> 18.9 us
    ppermute x6, waiting for transfers between devices: 44.8 us -> 33.7 us  [east(): return lax.ppermute(value, 'dp', EAST)]
    add x0 -> x1, other arithmetic: none -> 4.52 us  [local(): new_second = 0.95 * (second * (1.0 / SECOND_UNIT)) + 0.05 * grad * grad]
    ppermute x6, waiting for transfers between devices: 70 us -> 66.3 us  [west(): return lax.ppermute(value, 'dp', WEST)]
    unnamed x31 -> x35, local copies, waits for them, and re-layouts: 6.42 us -> 9.76 us
  transfers between devices with their start and end apart: 19 -> 19, of which waited for: 8 -> 8; matrix products, arithmetic and copies ran while one was open for 15% -> 21% of each run, Pallas kernels for 1% -> 1%
where the time goes in v1:
time: 278 us; the launch traced here: 277 us
  waiting for transfers between devices  117 us (42%)
  starting transfers between devices  67.4 us (24%)
  other arithmetic  43 us (15%)
  local copies, waits for them, and re-layouts  18.9 us (7%)
  between operations  15.1 us (5%)
  matrix products  12.7 us (5%)
  Pallas kernels  2.82 us (1%)
    ppermute x6, waiting for transfers between devices, west(): return lax.ppermute(value, 'dp', WEST)  66.3 us
    all_to_all x1, starting transfers between devices, local(): lax.all_to_all(packed, ('dp', 'mp'), split_axis=1, concat_axis=1, tiled=T...  38.4 us
    ppermute x6, waiting for transfers between devices, east(): return lax.ppermute(value, 'dp', EAST)  33.7 us
    ppermute x4, waiting for transfers between devices, across(): return lax.ppermute(value, 'dp', ACROSS)  17.2 us
    ppermute x6, starting transfers between devices, west(): return lax.ppermute(value, 'dp', WEST)  16.4 us
    dynamic_update_slice x9, other arithmetic, local(): out = lax.dynamic_update_slice(out, wide(values), (spot(dx, flip) + at, 0))  14.5 us
    dot_general x8, matrix products, product(): lax.dot_general(left, values, (((1,), (0,)), ((), ())), preferred_element...  12.7 us
    ppermute x4, starting transfers between devices, across(): return lax.ppermute(value, 'dp', ACROSS)  9.87 us
  transfers between devices with their start and end apart: 19, of which 8 were waited for; matrix products, arithmetic and copies ran while one was open for 21% of the time, Pallas kernels for 1%

profile of v1, /device:TPU:0, one launch (start us, length us, event | category | flops | bytes accessed | tf_op | source)
XLA Modules:
  0.0 277.1 jit_solution(10042810361636315647)
XLA Ops:
  9.7 2.1 copy.78
  19.1 4.1 %pad_maximum_fusion = f16[8,4,16,3584]{3,1,2,0:T(4,128)(2,1)} fusion(f16[8,4,16,896]{3,1,2,0:T(4,128)(2,1)S(1)} %copy.47, f16[8,4,16,896]{3,1,2,0:T(4,128)(2,1)S(1)} %copy.46, f16[8,4,16,896]{3,1,2,0:T(4,128)(2,1)S(1)} %copy.45, f16[8,4,16,896]{3,1,2,0:T(4,128)(2,1)S(1)} %copy.44), kind=kLoop, calls=%fused_computation | loop fusion | flops 5505024 | bytes 7340032 | tf_op jit(solution)/shard_map/concatenate | solution.py:133
  23.2 38.4 %all-to-all-start = ((f16[4,128,3584]{2,0,1:T(4,128)(2,1)}), f16[4,128,3584]{2,0,1:T(4,128)(2,1)}, u32[]{:S(2)}, u32[]{:S(2)}) async-start(f16[4,128,3584]{2,0,1:T(4,128)(2,1)} %bitcast.136), calls=%async_computation | async-start | bytes 7340032 | tf_op jit(solution)/shard_map/all_to_all | solution.py:135
  63.0 2.1 collective-permute-start.2
  65.9 2.4 collective-permute-start.1
  68.4 53.6 %collective-permute-done.2 = bf16[512,896]{1,0:T(8,128)(2,1)S(1)} collective-permute-done((bf16[512,896]{1,0:T(8,128)(2,1)}, bf16[512,896]{1,0:T(8,128)(2,1)S(1)}, u32[]{:S(2)}, u32[]{:S(2)}) %collective-permute-start.2) | collective-permute-done | bytes 917536 | tf_op jit(solution)/shard_map/ppermute | solution.py:48
  122.0 2.2 collective-permute-start.6
  124.9 17.9 %collective-permute-done.4 = bf16[512,896]{1,0:T(8,128)(2,1)} collective-permute-done((bf16[512,896]{1,0:T(8,128)(2,1)}, bf16[512,896]{1,0:T(8,128)(2,1)}, u32[]{:S(2)}, u32[]{:S(2)}) %collective-permute-start.4) | collective-permute-done | bytes 917536 | tf_op jit(solution)/shard_map/ppermute | solution.py:44
  142.8 2.8 %pad_maximum_fusion.2 = bf16[1024,896]{1,0:T(8,128)(2,1)} fusion(bf16[512,896]{1,0:T(8,128)(2,1)} %collective-permute-done.4, bf16[512,896]{1,0:T(8,128)(2,1)} %collective-permute-done.3), kind=kLoop, calls=%fused_computation.15 | loop fusion | flops 3670016 | bytes 3670016 | tf_op jit(solution)/shard_map/concatenate | solution.py:116
  145.6 2.6 pad_maximum_fusion.1
  148.1 12.7 %collective-permute-done.6 = bf16[512,896]{1,0:T(8,128)(2,1)} collective-permute-done((bf16[512,896]{1,0:T(8,128)(2,1)S(1)}, bf16[512,896]{1,0:T(8,128)(2,1)}, u32[]{:S(2)}, u32[]{:S(2)}) %collective-permute-start.6) | collective-permute-done | bytes 917536 | tf_op jit(solution)/shard_map/ppermute | solution.py:48
  162.0 2.9 %pad_maximum_fusion.3 = bf16[1024,896]{1,0:T(8,128)(2,1)} fusion(bf16[512,896]{1,0:T(8,128)(2,1)} %collective-permute-done.6, bf16[512,896]{1,0:T(8,128)(2,1)} %collective-permute-done.5), kind=kLoop, calls=%fused_computation.16 | loop fusion | flops 3670016 | bytes 3670016 | tf_op jit(solution)/shard_map/concatenate | solution.py:115
  164.9 3.5 %fusion.38 = (f16[4,128,896]{2,0,1:T(4,128)(2,1)S(1)}, f16[4,128,896]{2,0,1:T(4,128)(2,1)S(1)}, f16[4,128,896]{2,0,1:T(4,128)(2,1)S(1)}, f16[4,128,896]{2,0,1:T(4,128)(2,1)S(1)}) fusion(f16[4,128,3584]{2,0,1:T(4,128)(2,1)} %all-to-all-done), kind=kLoop, calls=%fused_computation.77 | loop fusion | bytes 7340032 | tf_op jit(solution)/shard_map/slice | solution.py:137
  169.8 2.4 fusion.33
  172.2 3.2 %fusion.22 = f32[896,2,256]{0,2,1:T(8,128)S(1)} fusion(bf16[1024,896]{1,0:T(8,128)(2,1)} %pad_maximum_fusion.2, bf16[4,4,1024,256]{3,2,1,0:T(8,128)(2,1)} %bitcast.148), kind=kOutput, calls=%fused_computation.39 | convolution fusion | flops 939524096 | bytes 4718592 | tf_op jit(solution)/shard_map/dot_general | solution.py:145
  182.8 3.3 %collective-permute-start.7 = (f16[512,896]{1,0:T(8,128)(2,1)S(1)}, f16[512,896]{1,0:T(8,128)(2,1)S(1)}, u32[]{:S(2)}, u32[]{:S(2)}) collective-permute-start(f16[512,896]{1,0:T(8,128)(2,1)S(1)} %bitcast.156), channel_id=1, source_target_pairs={{0,16},{16,0},{32,48},{48,32},{64,80},{80,64},{96,112},{112,96},{1... | collective-permute-start | bytes 2752520 | tf_op jit(solution)/shard_map/ppermute | solution.py:52
  190.2 16.3 %collective-permute-done.7 = f16[512,896]{1,0:T(8,128)(2,1)S(1)} collective-permute-done((f16[512,896]{1,0:T(8,128)(2,1)S(1)}, f16[512,896]{1,0:T(8,128)(2,1)S(1)}, u32[]{:S(2)}, u32[]{:S(2)}) %collective-permute-start.7) | collective-permute-done | bytes 917536 | tf_op jit(solution)/shard_map/ppermute | solution.py:52
  206.5 2.9 %fusion.12 = f16[512,896]{1,0:T(8,128)(2,1)} fusion(f32[4,128,896]{2,1,0:T(8,128)S(1)} %copy-done.4, f32[4,128,896]{2,1,0:T(8,128)S(1)} %copy-done.3, f32[512,896]{1,0:T(8,128)S(1)} %bitcast.134, f16[512,896]{1,0:T(8,128)(2,1)S(1)} %collective-permute-done.7, f32[]{:T(128)} %bitcast.29, f32[]{:T(128)} %bitcast.27, f16[4,128,896]{2,1,0:T(8,128)(2,1)S(1)} %copy-done.2, ...), kind=kLoop, calls=%fused_computation.24 | loop fusion | flops 9633792 | bytes 9175048 | tf_op jit(solution)/shard_map/convert_element_type | solution.py:163
  209.5 3.2 %collective-permute-start.9 = (f16[512,896]{1,0:T(8,128)(2,1)}, f16[512,896]{1,0:T(8,128)(2,1)}, u32[]{:S(2)}, u32[]{:S(2)}) collective-permute-start(f16[512,896]{1,0:T(8,128)(2,1)} %fusion.12), channel_id=1, source_target_pairs={{0,96},{16,112},{32,0},{48,16},{64,32},{80,48},{96,64},{112,80},{1... | collective-permute-start | bytes 2752520 | tf_op jit(solution)/shard_map/ppermute | solution.py:48
  212.7 3.0 %collective-permute-start.10 = (f16[512,896]{1,0:T(8,128)(2,1)}, f16[512,896]{1,0:T(8,128)(2,1)}, u32[]{:S(2)}, u32[]{:S(2)}) collective-permute-start(f16[512,896]{1,0:T(8,128)(2,1)} %fusion.12), channel_id=1, source_target_pairs={{0,16},{16,0},{32,48},{48,32},{64,80},{80,64},{96,112},{112,96},{1... | collective-permute-start | bytes 2752520 | tf_op jit(solution)/shard_map/ppermute | solution.py:52
  215.7 2.2 bitcast_convert_fusion
  217.9 2.6 convert_multiply_fusion.refs_0_
  220.5 2.8 %shard_map.85 = f32[4096,896]{1,0:T(8,128)} custom-call(s32[1]{0:T(128)} %bitcast.31.row_ref, f32[512,896]{1,0:T(8,128)} %convert_multiply_fusion.refs_0_), custom_call_target="tpu_custom_call" | custom-call | tf_op jit(solution)/shard_map/pallas_call | solution.py:71
  223.4 4.5 %fusion.8 = (f32[512,896]{1,0:T(8,128)}, f32[512,896]{1,0:T(8,128)}) fusion(f32[512,896]{1,0:T(8,128)} %get-tuple-element.10, f32[512,896]{1,0:T(8,128)S(1)} %bitcast.135, f16[512,896]{1,0:T(8,128)(2,1)S(1)} %copy-done.6, f32[512,896]{1,0:T(8,128)} %get-tuple-element.7), kind=kLoop, calls=%fused_computation.13 | loop fusion | flops 4587520 | bytes 10092544 | tf_op jit(solution)/shard_map/add | solution.py:167
  227.9 4.2 %collective-permute-done.8 = f16[512,896]{1,0:T(8,128)(2,1)} collective-permute-done((f16[512,896]{1,0:T(8,128)(2,1)}, f16[512,896]{1,0:T(8,128)(2,1)}, u32[]{:S(2)}, u32[]{:S(2)}) %collective-permute-start.8) | collective-permute-done | bytes 917536 | tf_op jit(solution)/shard_map/ppermute | solution.py:44
  234.4 3.3 %collective-permute-start.12 = (f16[256,896]{1,0:T(8,128)(2,1)S(1)}, f16[256,896]{1,0:T(8,128)(2,1)S(1)}, u32[]{:S(2)}, u32[]{:S(2)}) collective-permute-start(f16[256,896]{1,0:T(8,128)(2,1)S(1)} %slice.79), channel_id=1, source_target_pairs={{0,96},{16,112},{32,0},{48,16},{64,32},{80,48},{96,64},{112,80},{1... | collective-permute-start | bytes 1376264 | tf_op jit(solution)/shard_map/ppermute | solution.py:48
  237.7 3.2 %collective-permute-start.14 = (f16[512,896]{1,0:T(8,128)(2,1)}, f16[512,896]{1,0:T(8,128)(2,1)S(1)}, u32[]{:S(2)}, u32[]{:S(2)}) collective-permute-start(f16[512,896]{1,0:T(8,128)(2,1)} %collective-permute-done.10), channel_id=1, source_target_pairs={{0,96},{16,112},{32,0},{48,16},{64,32},{80,48},{96,64},{112,80},{1... | collective-permute-start | bytes 2752520 | tf_op jit(solution)/shard_map/ppermute | solution.py:48
  240.9 2.6 multiply_dynamic-update-slice_fusion.4
  243.5 2.6 multiply_dynamic-update-slice_fusion.3
  246.0 2.6 multiply_dynamic-update-slice_fusion.2
  248.6 3.0 %collective-permute-start.15 = (f16[256,896]{1,0:T(8,128)(2,1)S(1)}, f16[256,896]{1,0:T(8,128)(2,1)S(1)}, u32[]{:S(2)}, u32[]{:S(2)}) collective-permute-start(f16[256,896]{1,0:T(8,128)(2,1)S(1)} %collective-permute-done.11), channel_id=1, source_target_pairs={{0,16},{16,0},{32,48},{48,32},{64,80},{80,64},{96,112},{112,96},{1... | collective-permute-start | bytes 1376264 | tf_op jit(solution)/shard_map/ppermute | solution.py:52
  254.1 10.4 %collective-permute-done.13 = f16[512,896]{1,0:T(8,128)(2,1)S(1)} collective-permute-done((f16[512,896]{1,0:T(8,128)(2,1)}, f16[512,896]{1,0:T(8,128)(2,1)S(1)}, u32[]{:S(2)}, u32[]{:S(2)}) %collective-permute-start.13) | collective-permute-done | bytes 917536 | tf_op jit(solution)/shard_map/ppermute | solution.py:44
  (81 shorter events, 36.5 us)
Async XLA Ops:
  7.2 165.0 %all-gather.2.cloned.1.call-start = ((), (), s32[]{:S(2)}) async-start(), calls=%async_computation.1 | async-start | bytes 8912896 | tf_op jit(solution)/shard_map/all_gather | solution.py:111
  7.2 1.7 collective-permute-start
  8.9 0.8 copy-start.12
  13.8 1.5 copy-start.8
  16.0 1.5 copy-start.9
  23.2 38.4 %copy-start = (bf16[1024,896]{1,0:T(8,128)(2,1)S(1)}, bf16[1024,896]{1,0:T(8,128)(2,1)}, u32[]{:S(2)}) copy-start(bf16[1024,896]{1,0:T(8,128)(2,1)} %param.7) | copy-start | bytes 5505028
  23.2 141.7 %all-to-all-start = ((f16[4,128,3584]{2,0,1:T(4,128)(2,1)}), f16[4,128,3584]{2,0,1:T(4,128)(2,1)}, u32[]{:S(2)}, u32[]{:S(2)}) async-start(f16[4,128,3584]{2,0,1:T(4,128)(2,1)} %bitcast.136), calls=%async_computation | async-start | bytes 7340032 | tf_op jit(solution)/shard_map/all_to_all | solution.py:135
  63.0 59.0 %collective-permute-start.2 = (bf16[512,896]{1,0:T(8,128)(2,1)}, bf16[512,896]{1,0:T(8,128)(2,1)S(1)}, u32[]{:S(2)}, u32[]{:S(2)}) collective-permute-start(bf16[512,896]{1,0:T(8,128)(2,1)} %get-tuple-element.22), channel_id=1, source_target_pairs={{0,96},{16,112},{32,0},{48,16},{64,32},{80,48},{96,64},{112,80},{1... | collective-permute-start | bytes 2752520 | tf_op jit(solution)/shard_map/ppermute | solution.py:48
  65.1 59.0 %collective-permute-start.3 = (bf16[512,896]{1,0:T(8,128)(2,1)}, bf16[512,896]{1,0:T(8,128)(2,1)}, u32[]{:S(2)}, u32[]{:S(2)}) collective-permute-start(bf16[512,896]{1,0:T(8,128)(2,1)} %get-tuple-element.21), channel_id=1, source_target_pairs={{0,32},{16,48},{32,64},{48,80},{64,96},{80,112},{96,0},{112,16},{1... | collective-permute-start | bytes 2752520 | tf_op jit(solution)/shard_map/ppermute | solution.py:44
  65.1 77.7 %collective-permute-start.4 = (bf16[512,896]{1,0:T(8,128)(2,1)}, bf16[512,896]{1,0:T(8,128)(2,1)}, u32[]{:S(2)}, u32[]{:S(2)}) collective-permute-start(bf16[512,896]{1,0:T(8,128)(2,1)} %get-tuple-element.22), channel_id=1, source_target_pairs={{0,32},{16,48},{32,64},{48,80},{64,96},{80,112},{96,0},{112,16},{1... | collective-permute-start | bytes 2752520 | tf_op jit(solution)/shard_map/ppermute | solution.py:44
  65.9 79.7 %collective-permute-start.1 = (bf16[512,896]{1,0:T(8,128)(2,1)}, bf16[512,896]{1,0:T(8,128)(2,1)}, u32[]{:S(2)}, u32[]{:S(2)}) collective-permute-start(bf16[512,896]{1,0:T(8,128)(2,1)} %get-tuple-element.21), channel_id=1, source_target_pairs={{0,96},{16,112},{32,0},{48,16},{64,32},{80,48},{96,64},{112,80},{1... | collective-permute-start | bytes 2752520 | tf_op jit(solution)/shard_map/ppermute | solution.py:48
  122.0 38.9 %collective-permute-start.6 = (bf16[512,896]{1,0:T(8,128)(2,1)S(1)}, bf16[512,896]{1,0:T(8,128)(2,1)}, u32[]{:S(2)}, u32[]{:S(2)}) collective-permute-start(bf16[512,896]{1,0:T(8,128)(2,1)S(1)} %collective-permute-done.2), channel_id=1, source_target_pairs={{0,96},{16,112},{32,0},{48,16},{64,32},{80,48},{96,64},{112,80},{1... | collective-permute-start | bytes 2752520 | tf_op jit(solution)/shard_map/ppermute | solution.py:48
  124.1 37.9 %collective-permute-start.5 = (bf16[512,896]{1,0:T(8,128)(2,1)}, bf16[512,896]{1,0:T(8,128)(2,1)}, u32[]{:S(2)}, u32[]{:S(2)}) collective-permute-start(bf16[512,896]{1,0:T(8,128)(2,1)} %collective-permute-done.3), channel_id=1, source_target_pairs={{0,32},{16,48},{32,64},{48,80},{64,96},{80,112},{96,0},{112,16},{1... | collective-permute-start | bytes 2752520 | tf_op jit(solution)/shard_map/ppermute | solution.py:44
  172.2 4.2 %copy-start.7 = (bf16[16384,256]{1,0:T(8,128)(2,1)S(1)}, bf16[16384,256]{1,0:T(8,128)(2,1)}, u32[]{:S(2)}) copy-start(bf16[16384,256]{1,0:T(8,128)(2,1)} %all-gather.2.cloned.1.call-done) | copy-start | bytes 25165828
  172.2 4.8 %copy-start.11 = (bf16[1024,896]{1,0:T(8,128)(2,1)S(1)}, bf16[1024,896]{1,0:T(8,128)(2,1)}, u32[]{:S(2)}) copy-start(bf16[1024,896]{1,0:T(8,128)(2,1)} %pad_maximum_fusion.2) | copy-start | bytes 5505028
  178.3 1.5 copy-start.10
  179.8 1.5 copy-start.1
  182.8 23.8 %collective-permute-start.7 = (f16[512,896]{1,0:T(8,128)(2,1)S(1)}, f16[512,896]{1,0:T(8,128)(2,1)S(1)}, u32[]{:S(2)}, u32[]{:S(2)}) collective-permute-start(f16[512,896]{1,0:T(8,128)(2,1)S(1)} %bitcast.156), channel_id=1, source_target_pairs={{0,16},{16,0},{32,48},{48,32},{64,80},{80,64},{96,112},{112,96},{1... | collective-permute-start | bytes 2752520 | tf_op jit(solution)/shard_map/ppermute | solution.py:52
  188.7 17.9 %copy-start.2 = (f16[4,128,896]{2,1,0:T(8,128)(2,1)S(1)}, f16[4,128,896]{2,1,0:T(8,128)(2,1)}, u32[]{:S(2)}) copy-start(f16[4,128,896]{2,1,0:T(8,128)(2,1)} %copy.63) | copy-start | bytes 2752516
  188.7 17.9 %copy-start.3 = (f32[4,128,896]{2,1,0:T(8,128)S(1)}, f32[4,128,896]{2,1,0:T(8,128)}, u32[]{:S(2)}) copy-start(f32[4,128,896]{2,1,0:T(8,128)} %get-tuple-element.17) | copy-start | bytes 5505028
  188.7 17.9 %copy-start.4 = (f32[4,128,896]{2,1,0:T(8,128)S(1)}, f32[4,128,896]{2,1,0:T(8,128)}, u32[]{:S(2)}) copy-start(f32[4,128,896]{2,1,0:T(8,128)} %get-tuple-element.18) | copy-start | bytes 5505028
  206.5 2.9 %copy-start.5 = (f16[512,896]{1,0:T(8,128)(2,1)}, f16[512,896]{1,0:T(8,128)(2,1)S(1)}, u32[]{:S(2)}) copy-start(f16[512,896]{1,0:T(8,128)(2,1)S(1)} %collective-permute-done.7) | copy-start | bytes 2752516
  209.4 22.6 %collective-permute-start.8 = (f16[512,896]{1,0:T(8,128)(2,1)}, f16[512,896]{1,0:T(8,128)(2,1)}, u32[]{:S(2)}, u32[]{:S(2)}) collective-permute-start(f16[512,896]{1,0:T(8,128)(2,1)} %fusion.12), channel_id=1, source_target_pairs={{0,32},{16,48},{32,64},{48,80},{64,96},{80,112},{96,0},{112,16},{1... | collective-permute-start | bytes 2752520 | tf_op jit(solution)/shard_map/ppermute | solution.py:44
  209.5 23.7 %collective-permute-start.9 = (f16[512,896]{1,0:T(8,128)(2,1)}, f16[512,896]{1,0:T(8,128)(2,1)}, u32[]{:S(2)}, u32[]{:S(2)}) collective-permute-start(f16[512,896]{1,0:T(8,128)(2,1)} %fusion.12), channel_id=1, source_target_pairs={{0,96},{16,112},{32,0},{48,16},{64,32},{80,48},{96,64},{112,80},{1... | collective-permute-start | bytes 2752520 | tf_op jit(solution)/shard_map/ppermute | solution.py:48
  212.7 25.0 %collective-permute-start.10 = (f16[512,896]{1,0:T(8,128)(2,1)}, f16[512,896]{1,0:T(8,128)(2,1)}, u32[]{:S(2)}, u32[]{:S(2)}) collective-permute-start(f16[512,896]{1,0:T(8,128)(2,1)} %fusion.12), channel_id=1, source_target_pairs={{0,16},{16,0},{32,48},{48,32},{64,80},{80,64},{96,112},{112,96},{1... | collective-permute-start | bytes 2752520 | tf_op jit(solution)/shard_map/ppermute | solution.py:52
  220.5 2.8 %copy-start.6 = (f16[512,896]{1,0:T(8,128)(2,1)S(1)}, f16[512,896]{1,0:T(8,128)(2,1)}, u32[]{:S(2)}) copy-start(f16[512,896]{1,0:T(8,128)(2,1)} %copy-done.5) | copy-start | bytes 2752516
  233.2 15.4 %collective-permute-start.11 = (f16[256,896]{1,0:T(8,128)(2,1)S(1)}, f16[256,896]{1,0:T(8,128)(2,1)S(1)}, u32[]{:S(2)}, u32[]{:S(2)}) collective-permute-start(f16[256,896]{1,0:T(8,128)(2,1)S(1)} %slice.78), channel_id=1, source_target_pairs={{0,32},{16,48},{32,64},{48,80},{64,96},{80,112},{96,0},{112,16},{1... | collective-permute-start | bytes 1376264 | tf_op jit(solution)/shard_map/ppermute | solution.py:44
  234.4 17.3 %collective-permute-start.12 = (f16[256,896]{1,0:T(8,128)(2,1)S(1)}, f16[256,896]{1,0:T(8,128)(2,1)S(1)}, u32[]{:S(2)}, u32[]{:S(2)}) collective-permute-start(f16[256,896]{1,0:T(8,128)(2,1)S(1)} %slice.79), channel_id=1, source_target_pairs={{0,96},{16,112},{32,0},{48,16},{64,32},{80,48},{96,64},{112,80},{1... | collective-permute-start | bytes 1376264 | tf_op jit(solution)/shard_map/ppermute | solution.py:48
  237.7 26.9 %collective-permute-start.13 = (f16[512,896]{1,0:T(8,128)(2,1)}, f16[512,896]{1,0:T(8,128)(2,1)S(1)}, u32[]{:S(2)}, u32[]{:S(2)}) collective-permute-start(f16[512,896]{1,0:T(8,128)(2,1)} %collective-permute-done.10), channel_id=1, source_target_pairs={{0,32},{16,48},{32,64},{48,80},{64,96},{80,112},{96,0},{112,16},{1... | collective-permute-start | bytes 2752520 | tf_op jit(solution)/shard_map/ppermute | solution.py:44
  237.7 28.3 %collective-permute-start.14 = (f16[512,896]{1,0:T(8,128)(2,1)}, f16[512,896]{1,0:T(8,128)(2,1)S(1)}, u32[]{:S(2)}, u32[]{:S(2)}) collective-permute-start(f16[512,896]{1,0:T(8,128)(2,1)} %collective-permute-done.10), channel_id=1, source_target_pairs={{0,96},{16,112},{32,0},{48,16},{64,32},{80,48},{96,64},{112,80},{1... | collective-permute-start | bytes 2752520 | tf_op jit(solution)/shard_map/ppermute | solution.py:48
  248.6 18.7 %collective-permute-start.15 = (f16[256,896]{1,0:T(8,128)(2,1)S(1)}, f16[256,896]{1,0:T(8,128)(2,1)S(1)}, u32[]{:S(2)}, u32[]{:S(2)}) collective-permute-start(f16[256,896]{1,0:T(8,128)(2,1)S(1)} %collective-permute-done.11), channel_id=1, source_target_pairs={{0,16},{16,0},{32,48},{48,32},{64,80},{80,64},{96,112},{112,96},{1... | collective-permute-start | bytes 1376264 | tf_op jit(solution)/shard_map/ppermute | solution.py:52
  251.7 17.6 %collective-permute-start.16 = (f16[256,896]{1,0:T(8,128)(2,1)S(1)}, f16[256,896]{1,0:T(8,128)(2,1)S(1)}, u32[]{:S(2)}, u32[]{:S(2)}) collective-permute-start(f16[256,896]{1,0:T(8,128)(2,1)S(1)} %collective-permute-done.12), channel_id=1, source_target_pairs={{0,16},{16,0},{32,48},{48,32},{64,80},{80,64},{96,112},{112,96},{1... | collective-permute-start | bytes 1376264 | tf_op jit(solution)/shard_map/ppermute | solution.py:52
Sparse Core Ops, SparseCore 0:
  9.9 121.1 all-gather.1
